TPU v7x, 256 devices: a whole 4x4x8 slice. The times are simulated.
256 devices in a mesh: seq: 64 (over z, x, core), head: 4 (over y).
Axes of the slice: x: 4, y: 4, z: 8, core: 2. Of those that a mesh axis runs over, the one named last changes fastest.
Arguments:
- qk: bfloat16 [65536, 2048], P('seq', 'head'), may hold values from -8 to 8
- values: bfloat16 [65536, 2048], P('seq', 'head'), may hold values from -6 to 6
- out_weight: bfloat16 [2048, 2048], P('head'), may hold values from -0.125 to 0.125
- out_cotangent: bfloat16 [65536, 2048], P('seq', 'head'), may hold values from -6 to 6
- cluster_ids: int32 [512, 16], P(None, 'head'), may hold values from 0 to 127, as said below
Outputs:
- output: bfloat16 [65536, 2048], P('seq', 'head')
- grad_qk: bfloat16 [65536, 2048], P('seq', 'head')
- grad_values: bfloat16 [65536, 2048], P('seq', 'head')
Inputs may be any that keep to these rules, and one draw needn't show every extreme that they name: `cluster_ids`: call c // 2 the owner of cluster c. Over the blocks of one seq index and the heads of one head index, at most 2 name clusters of one owner, and exactly 2 for some owner. For every head, the clusters of each owner hold exactly 8 blocks together, and some cluster holds all 8.
All inputs are finite; a program needn't handle non-finite values.
Results may differ from a plain program's by a relative error of at most 0.013.
Values may be sent and summed in bfloat16 or wider, within the bound.
A program may use at most 128 MiB of HBM per device.

v0:
```python
import jax
import jax.numpy as jnp
from jax import lax
from jax.sharding import PartitionSpec as P

BLOCK = 128
CL_OWN = 2
NEG_FILL = -1e30


def unit_forward(tokens_x, tokens_v, group):
    row_count = tokens_x.shape[0]
    block_rows = row_count // group.shape[0]
    inv_root = tokens_x.shape[1] ** (-0.5)
    scores = (
        jnp.einsum("rd,cd->rc", tokens_x, tokens_x, preferred_element_type=jnp.float32) * inv_root
    )
    row_group = jnp.repeat(group, block_rows)
    position = jnp.arange(row_count)
    allowed = (row_group[:, None] == row_group[None, :]) & (position[:, None] != position[None, :])
    scores = jnp.where(allowed, scores, NEG_FILL)
    row_max = jnp.max(scores, axis=1, keepdims=True)
    raised = jnp.exp(scores - row_max)
    weights = raised / jnp.sum(raised, axis=1, keepdims=True)
    attended = jnp.einsum(
        "rc,cd->rd", weights.astype(jnp.bfloat16), tokens_v, preferred_element_type=jnp.float32
    )
    return (weights, attended)


def unit_backward(tokens_x, tokens_v, grad_rows, weights, attended):
    inv_root = tokens_x.shape[1] ** (-0.5)
    grad_weights = jnp.einsum("rd,cd->rc", grad_rows, tokens_v, preferred_element_type=jnp.float32)
    row_delta = jnp.sum(grad_rows.astype(jnp.float32) * attended, axis=1, keepdims=True)
    grad_scores = weights * (grad_weights - row_delta)
    symmetric = (grad_scores + grad_scores.T).astype(jnp.bfloat16)
    grad_x = (
        jnp.einsum("rc,cd->rd", symmetric, tokens_x, preferred_element_type=jnp.float32) * inv_root
    ).astype(jnp.bfloat16)
    grad_v = jnp.einsum(
        "rc,rd->cd", weights.astype(jnp.bfloat16), grad_rows, preferred_element_type=jnp.float32
    ).astype(jnp.bfloat16)
    return (grad_x, grad_v)


def forward_unit(operands):
    tokens_x, tokens_v, group = operands
    return unit_forward(tokens_x, tokens_v, group)


def backward_unit(operands):
    tokens_x, tokens_v, grad_rows, weights, attended = operands
    return unit_backward(tokens_x, tokens_v, grad_rows, weights, attended)


def to_slots(local, packing, seq_count):
    blocks_here = packing.shape[1]
    heads_here = packing.shape[2]
    head_width = local.shape[1] // heads_here
    shaped = local.reshape(blocks_here, BLOCK, heads_here, head_width)
    packed = jnp.einsum(
        "ptk,trkd->prd", packing, shaped, preferred_element_type=jnp.float32
    ).astype(jnp.bfloat16)
    return packed.reshape(seq_count, -1, head_width)


def from_slots(arrived, packing):
    head_width = arrived.shape[-1]
    flat = arrived.reshape(packing.shape[0], BLOCK, head_width)
    placed = jnp.einsum("ptk,prd->trkd", packing, flat, preferred_element_type=jnp.float32).astype(
        jnp.bfloat16
    )
    return placed.reshape(packing.shape[1] * BLOCK, packing.shape[2] * head_width)


def to_units(arrived, picking, unit_count):
    head_width = arrived.shape[-1]
    flat = arrived.reshape(picking.shape[1], BLOCK, head_width)
    gathered = jnp.einsum("up,prd->urd", picking, flat, preferred_element_type=jnp.float32).astype(
        jnp.bfloat16
    )
    return gathered.reshape(unit_count, -1, head_width)


def from_units(results, picking, seq_count):
    head_width = results.shape[-1]
    flat = results.reshape(picking.shape[0], BLOCK, head_width)
    placed = jnp.einsum("up,urd->prd", picking, flat, preferred_element_type=jnp.float32).astype(
        jnp.bfloat16
    )
    return placed.reshape(seq_count, -1, head_width)


def model_output(attended, out_weight):
    partial_term = jnp.dot(attended, out_weight, preferred_element_type=jnp.float32)
    return lax.psum_scatter(
        partial_term.astype(jnp.bfloat16), "head", scatter_dimension=1, tiled=True
    )


def cotangent_heads(out_cotangent, out_weight):
    summed = jnp.einsum(
        "tn,kn->tk",
        lax.all_gather(out_cotangent, "head", axis=1, tiled=True),
        out_weight,
        preferred_element_type=jnp.float32,
    )
    return summed.astype(jnp.bfloat16)


def per_device(qk, values, out_weight, out_cotangent, cluster_ids):
    seq_count = lax.axis_size("seq")
    my_seq = lax.axis_index("seq")
    block_count = cluster_ids.shape[0]
    heads_here = cluster_ids.shape[1]
    blocks_here = qk.shape[0] // BLOCK
    item_count = blocks_here * heads_here
    per_peer = max(2, (item_count + seq_count - 1) // seq_count)
    slot_total = seq_count * per_peer
    owners = cluster_ids // CL_OWN
    item_owner = owners.reshape(seq_count, item_count)
    item_order = jnp.arange(item_count)
    before = item_order[None, :] < item_order[:, None]
    same_owner = item_owner[:, :, None] == item_owner[:, None, :]
    rank_sent = jnp.sum((same_owner & before[None, :, :]).astype(jnp.int32), axis=2)
    slot_index = item_owner * per_peer + rank_sent
    my_slots = lax.dynamic_index_in_dim(slot_index, my_seq, 0, keepdims=False)
    slot_range = jnp.arange(slot_total, dtype=jnp.int32)
    packing = (
        (slot_range[:, None] == my_slots[None, :])
        .astype(jnp.bfloat16)
        .reshape(slot_total, blocks_here, heads_here)
    )
    source_seq = jnp.arange(seq_count, dtype=jnp.int32)[:, None]
    arrival_slot = source_seq * per_peer + rank_sent
    received = (owners == my_seq).T.astype(jnp.int32)
    source_slot = arrival_slot.reshape(block_count, heads_here).T
    position = jnp.cumsum(received, axis=1) - received
    places = jnp.arange(blocks_here, dtype=jnp.int32)
    chosen = (received[:, None, :] == 1) & (position[:, None, :] == places[None, :, None])
    unit_slot = jnp.sum(jnp.where(chosen, source_slot[:, None, :], 0), axis=2)
    unit_group = jnp.sum(jnp.where(chosen, cluster_ids.T[:, None, :], 0), axis=2)
    picking = (unit_slot.reshape(-1)[:, None] == slot_range[None, :]).astype(jnp.bfloat16)
    send_x = to_slots(qk, packing, seq_count)
    send_v = to_slots(values, packing, seq_count)
    arrived_x, arrived_v = (
        lax.all_to_all(send_x, "seq", split_axis=0, concat_axis=0, tiled=True),
        lax.all_to_all(send_v, "seq", split_axis=0, concat_axis=0, tiled=True),
    )
    unit_x = to_units(arrived_x, picking, heads_here)
    unit_v = to_units(arrived_v, picking, heads_here)
    weights, unit_att = lax.map(forward_unit, (unit_x, unit_v, unit_group))
    home_att = lax.all_to_all(
        from_units(unit_att.astype(jnp.bfloat16), picking, seq_count),
        "seq",
        split_axis=0,
        concat_axis=0,
        tiled=True,
    )
    attended = from_slots(home_att, packing)
    output = model_output(attended, out_weight)
    grad_attended = cotangent_heads(out_cotangent, out_weight)
    arrived_g = lax.all_to_all(
        to_slots(grad_attended, packing, seq_count), "seq", split_axis=0, concat_axis=0, tiled=True
    )
    unit_g = to_units(arrived_g, picking, heads_here)
    unit_gx, unit_gv = lax.map(backward_unit, (unit_x, unit_v, unit_g, weights, unit_att))
    home_gx, home_gv = (
        lax.all_to_all(
            from_units(unit_gx, picking, seq_count), "seq", split_axis=0, concat_axis=0, tiled=True
        ),
        lax.all_to_all(
            from_units(unit_gv, picking, seq_count), "seq", split_axis=0, concat_axis=0, tiled=True
        ),
    )
    grad_qk = from_slots(home_gx, packing)
    grad_values = from_slots(home_gv, packing)
    return (output, grad_qk, grad_values)


def solution(mesh):
    return jax.shard_map(
        per_device,
        mesh=mesh,
        in_specs=(
            P("seq", "head"),
            P("seq", "head"),
            P("head", None),
            P("seq", "head"),
            P(None, "head"),
        ),
        out_specs=(P("seq", "head"), P("seq", "head"), P("seq", "head")),
        check_vma=False,
    )
```

profile of v0, /device:TPU:16, one launch (start us, length us, event | category | flops | bytes accessed | tf_op | source)
XLA Modules:
  0.0 683.7 jit_solution(4577155340845065639)
XLA Ops:
  11.8 4.6 copy.60
  16.4 12.2 %all-to-all-start = ((bf16[64,256,128]{2,1,0:T(8,128)(2,1)}), bf16[64,256,128]{2,1,0:T(8,128)(2,1)}, u32[]{:S(2)}, u32[]{:S(2)}) async-start(bf16[64,256,128]{2,1,0:T(8,128)(2,1)} %bitcast.193), calls=%async_computation | async-start | bytes 8388608 | tf_op jit(solution)/shard_map/all_to_all | solution.py:147
  31.4 4.7 copy.64
  36.0 88.8 %all-to-all-done = bf16[64,256,128]{2,1,0:T(8,128)(2,1)} async-done(((bf16[64,256,128]{2,1,0:T(8,128)(2,1)}), bf16[64,256,128]{2,1,0:T(8,128)(2,1)}, u32[]{:S(2)}, u32[]{:S(2)}) %all-to-all-start) | async-done | bytes 4194336 | tf_op jit(solution)/shard_map/all_to_all | solution.py:147
  124.8 5.8 all-to-all-start.1
  134.1 50.2 %all-gather.2.cloned.1.call-done = bf16[1024,2048]{1,0:T(8,128)(2,1)} async-done(((bf16[1024,512]{1,0:T(8,128)(2,1)}), bf16[1024,2048]{1,0:T(8,128)(2,1)}) %all-gather.2.cloned.1.call-update) | async-done | bytes 4194320 | tf_op jit(solution)/shard_map/all_gather | solution.py:104
  184.3 5.5 convolution_convert_fusion.4
  192.6 4.6 copy.73
  197.2 4.8 fusion.70
  202.4 24.5 %all-to-all-done.1 = bf16[64,256,128]{2,1,0:T(8,128)(2,1)} async-done(((bf16[64,256,128]{2,1,0:T(8,128)(2,1)}), bf16[64,256,128]{2,1,0:T(8,128)(2,1)}, u32[]{:S(2)}, u32[]{:S(2)}) %all-to-all-start.1) | async-done | bytes 4194336 | tf_op jit(solution)/shard_map/all_to_all | solution.py:148
  226.9 6.1 all-to-all-start.3
  233.0 4.8 fusion.73
  239.2 27.8 %while.24 = (s32[]{:T(128)}, f32[4,1024,1024]{1,2,0:T(8,128)}, f32[4,1024,128]{2,1,0:T(8,128)}, s32[4,8]{1,0:T(4,128)S(1)}, bf16[4,1024,128]{2,1,0:T(8,128)(2,1)S(1)}, /*index=5*/bf16[4,1024,128]{2,1,0:T(8,128)(2,1)}, s32[]{:T(128)}) while((s32[]{:T(128)}, f32[4,1024,1024]{1,2,0:T(8,128)}, f32[4,1024,128]{2,1,0:T(8,128)}, ...), condition=%wide.region_8.9_spmd, body=%wide.region_5.8_spmd.sunk | while | flops 550500352 | bytes 22062772 | solution.py:152
  241.0 2.5 bitcast_dynamic-update-slice_fusion.2
  243.5 2.6 fusion.160
  247.9 2.5 bitcast_dynamic-update-slice_fusion.2
  250.5 2.6 fusion.160
  254.9 2.5 bitcast_dynamic-update-slice_fusion.2
  257.4 2.6 fusion.160
  261.8 2.5 bitcast_dynamic-update-slice_fusion.2
  264.4 2.6 fusion.160
  266.9 2.1 convert_element_type.93
  270.4 4.7 copy.68
  275.1 54.1 %all-to-all-done.3 = bf16[64,256,128]{2,1,0:T(8,128)(2,1)} async-done(((bf16[64,256,128]{2,1,0:T(8,128)(2,1)}), bf16[64,256,128]{2,1,0:T(8,128)(2,1)}, u32[]{:S(2)}, u32[]{:S(2)}) %all-to-all-start.3) | async-done | bytes 4194336 | tf_op jit(solution)/shard_map/all_to_all | solution.py:163
  329.2 5.8 all-to-all-start.2
  335.0 4.8 fusion.76
  340.3 112.8 %while.25 = (s32[]{:T(128)}, bf16[4,1024,128]{2,1,0:T(8,128)(2,1)}, bf16[4,1024,128]{2,1,0:T(8,128)(2,1)}, f32[4,1024,1024]{1,2,0:T(8,128)}, bf16[4,1024,128]{2,...) while((s32[]{:T(128)}, bf16[4,1024,128]{2,1,0:T(8,128)(2,1)}, ...), condition=%wide.region_12.13_spmd, body=%wide.region_10.12_spmd.sunk | while | flops 811334656 | bytes 65285248 | solution.py:167
  341.5 4.7 constant_dynamic-slice_fusion.3
  346.3 5.3 copy.159
  351.6 4.9 bitcast_multiply_fusion.3
  356.5 5.4 copy.160
  361.9 5.1 fusion.168
  367.0 1.5 fusion.169
  369.7 4.7 constant_dynamic-slice_fusion.3
  374.5 5.3 copy.159
  379.8 4.9 bitcast_multiply_fusion.3
  384.7 5.4 copy.160
  390.1 5.1 fusion.168
  395.2 1.5 fusion.169
  397.9 4.7 constant_dynamic-slice_fusion.3
  402.7 5.3 copy.159
  408.0 4.9 bitcast_multiply_fusion.3
  412.9 5.4 copy.160
  418.3 5.1 fusion.168
  423.4 1.5 fusion.169
  426.1 4.7 constant_dynamic-slice_fusion.3
  430.9 5.3 copy.159
  436.2 4.9 bitcast_multiply_fusion.3
  441.1 5.4 copy.160
  446.5 5.1 fusion.168
  453.1 2.6 convolution_convert_fusion.2
  455.7 4.7 copy.78
  460.4 10.9 %all-to-all-start.4 = ((bf16[64,256,128]{2,1,0:T(8,128)(2,1)}), bf16[64,256,128]{2,1,0:T(8,128)(2,1)}, u32[]{:S(2)}, u32[]{:S(2)}) async-start(bf16[64,256,128]{2,1,0:T(8,128)(2,1)} %bitcast.192), calls=%async_computation.5 | async-start | bytes 8388608 | tf_op jit(solution)/shard_map/all_to_all | solution.py:169
  471.2 2.6 convolution_convert_fusion.1
  473.8 4.7 copy.82
  478.5 88.9 %all-to-all-done.4 = bf16[64,256,128]{2,1,0:T(8,128)(2,1)} async-done(((bf16[64,256,128]{2,1,0:T(8,128)(2,1)}), bf16[64,256,128]{2,1,0:T(8,128)(2,1)}, u32[]{:S(2)}, u32[]{:S(2)}) %all-to-all-start.4) | async-done | bytes 4194336 | tf_op jit(solution)/shard_map/all_to_all | solution.py:169
  567.5 5.8 all-to-all-start.5
  573.3 4.8 fusion.94
  578.1 2.0 copy.71
  580.1 5.6 convolution_convert_fusion
  585.7 4.8 fusion.91
  591.0 78.5 %all-to-all-done.5 = bf16[64,256,128]{2,1,0:T(8,128)(2,1)} async-done(((bf16[64,256,128]{2,1,0:T(8,128)(2,1)}), bf16[64,256,128]{2,1,0:T(8,128)(2,1)}, u32[]{:S(2)}, u32[]{:S(2)}) %all-to-all-start.5) | async-done | bytes 4194336 | tf_op jit(solution)/shard_map/all_to_all | solution.py:172
  669.5 4.8 fusion.88
  674.7 1.7 copy_bitcast_fusion
  (85 shorter events, 31.7 us)
Async XLA Ops:
  7.2 177.1 %copy-start = (bf16[512,2048]{1,0:T(8,128)(2,1)S(1)}, bf16[512,2048]{1,0:T(8,128)(2,1)}, u32[]{:S(2)}) copy-start(bf16[512,2048]{1,0:T(8,128)(2,1)} %param.11) | copy-start | bytes 6291460
  9.0 182.1 %copy-start.3 = (s32[8,4]{0,1:T(4,128)}, s32[8,4]{0,1:T(4,128)S(1)}, u32[]{:S(2)}) copy-start(s32[8,4]{0,1:T(4,128)S(1)} %copy.58) | copy-start | bytes 388
  16.4 108.4 %all-to-all-start = ((bf16[64,256,128]{2,1,0:T(8,128)(2,1)}), bf16[64,256,128]{2,1,0:T(8,128)(2,1)}, u32[]{:S(2)}, u32[]{:S(2)}) async-start(bf16[64,256,128]{2,1,0:T(8,128)(2,1)} %bitcast.193), calls=%async_computation | async-start | bytes 8388608 | tf_op jit(solution)/shard_map/all_to_all | solution.py:147
  124.8 8.9 %copy-start.5 = (s32[512,4]{0,1:T(4,128)S(1)}, s32[512,4]{0,1:T(4,128)}, u32[]{:S(2)}) copy-start(s32[512,4]{0,1:T(4,128)} %param.13) | copy-start | bytes 24580
  124.8 102.0 %all-to-all-start.1 = ((bf16[64,256,128]{2,1,0:T(8,128)(2,1)}), bf16[64,256,128]{2,1,0:T(8,128)(2,1)}, u32[]{:S(2)}, u32[]{:S(2)}) async-start(bf16[64,256,128]{2,1,0:T(8,128)(2,1)} %bitcast.190), calls=%async_computation.1 | async-start | bytes 8388608 | tf_op jit(solution)/shard_map/all_to_all | solution.py:148
  130.6 53.7 %all-gather.2.cloned.1.call-start = ((), (), s32[]{:S(2)}) async-start(), calls=%async_computation.8 | async-start | bytes 5242880 | tf_op jit(solution)/shard_map/all_gather | solution.py:104
  226.9 102.3 %all-to-all-start.3 = ((bf16[64,256,128]{2,1,0:T(8,128)(2,1)}), bf16[64,256,128]{2,1,0:T(8,128)(2,1)}, u32[]{:S(2)}, u32[]{:S(2)}) async-start(bf16[64,256,128]{2,1,0:T(8,128)(2,1)} %bitcast.188), calls=%async_computation.4 | async-start | bytes 8388608 | tf_op jit(solution)/shard_map/all_to_all | solution.py:163
  266.9 3.5 copy-start.2
  329.2 131.2 %all-to-all-start.2 = ((bf16[64,256,128]{2,1,0:T(8,128)(2,1)}), bf16[64,256,128]{2,1,0:T(8,128)(2,1)}, u32[]{:S(2)}, u32[]{:S(2)}) async-start(bf16[64,256,128]{2,1,0:T(8,128)(2,1)} %bitcast.189), calls=%async_computation.2 | async-start | bytes 8388608 | tf_op jit(solution)/shard_map/all_to_all | solution.py:153
  361.9 5.1 copy-start.1
  390.1 5.1 copy-start.1
  418.3 5.1 copy-start.1
  446.5 5.1 copy-start.1
  460.4 107.1 %all-to-all-start.4 = ((bf16[64,256,128]{2,1,0:T(8,128)(2,1)}), bf16[64,256,128]{2,1,0:T(8,128)(2,1)}, u32[]{:S(2)}, u32[]{:S(2)}) async-start(bf16[64,256,128]{2,1,0:T(8,128)(2,1)} %bitcast.192), calls=%async_computation.5 | async-start | bytes 8388608 | tf_op jit(solution)/shard_map/all_to_all | solution.py:169
  567.4 5.9 copy-start.4
  567.5 102.0 %all-to-all-start.5 = ((bf16[64,256,128]{2,1,0:T(8,128)(2,1)}), bf16[64,256,128]{2,1,0:T(8,128)(2,1)}, u32[]{:S(2)}, u32[]{:S(2)}) async-start(bf16[64,256,128]{2,1,0:T(8,128)(2,1)} %bitcast.191), calls=%async_computation.6 | async-start | bytes 8388608 | tf_op jit(solution)/shard_map/all_to_all | solution.py:172
  573.3 103.2 %reduce-scatter.2.cloned.1.call-start = ((), (), s32[]{:S(2)}) async-start(), calls=%async_computation.7 | async-start | bytes 5242880 | tf_op jit(solution)/shard_map/reduce_scatter | solution.py:96
Sparse Core Ops, SparseCore 0:
  133.3 50.9 all-gather.1
  585.8 48.8 reduce-scatter.1
where the time goes:
time: 694 us; the launch traced here: 684 us
  waiting for transfers between devices  386 us (56%)
  matrix products  111 us (16%)
  local copies, waits for them, and re-layouts  102 us (15%)
  starting transfers between devices  46.9 us (7%)
  other arithmetic  22.8 us (3%)
  between operations  14.8 us (2%)
    all_to_all x1, waiting for transfers between devices, per_device(): lax.all_to_all(from_units(unit_gx, picking, seq_count), 'seq', split_axis...  88.9 us
    all_to_all x1, waiting for transfers between devices, per_device(): lax.all_to_all(send_x, 'seq', split_axis=0, concat_axis=0, tiled=True)  88.8 us
    all_to_all x1, waiting for transfers between devices, per_device(): lax.all_to_all(from_units(unit_gv, picking, seq_count), 'seq', split_axis...  78.5 us
    all_to_all x1, waiting for transfers between devices, per_device(): lax.all_to_all(to_slots(grad_attended, packing, seq_count), 'seq', split_...  54.1 us
    all_gather x1, waiting for transfers between devices, cotangent_heads(): lax.all_gather(out_cotangent, 'head', axis=1, tiled=True)  50.2 us
    dynamic_slice x8, local copies, waits for them, and re-layouts, per_device(): lax.map(backward_unit, (unit_x, unit_v, unit_g, weights, unit_att))  40.2 us
    all_to_all x1, waiting for transfers between devices, per_device(): lax.all_to_all(send_v, 'seq', split_axis=0, concat_axis=0, tiled=True)  24.5 us
    mul x4, local copies, waits for them, and re-layouts, unit_backward(): grad_scores = weights * (grad_weights - row_delta)  21.5 us
  transfers between devices with their start and end apart: 8, of which 6 were waited for; matrix products, arithmetic and copies ran while one was open for 33% of the time, Pallas kernels for 0%

commit v1 on v0

--- a/solution.py
+++ b/solution.py
@@ -6,6 +6,19 @@
 BLOCK = 128
 CL_OWN = 2
 NEG_FILL = -1e30
+
+
+def gather_around(x, axis, dim):
+    ways = lax.axis_size(axis)
+    up = [(d, (d + 1) % ways) for d in range(ways)]
+    down = [(d, (d - 1) % ways) for d in range(ways)]
+    earlier, later = ([x], [x])
+    for _ in range(ways // 2):
+        earlier.append(lax.ppermute(earlier[-1], axis, up))
+    for _ in range((ways - 1) // 2):
+        later.append(lax.ppermute(later[-1], axis, down))
+    line = jnp.concatenate([*earlier[::-1], *later[1:]], axis=dim)
+    return jnp.roll(line, (lax.axis_index(axis) - ways // 2) * x.shape[dim], axis=dim)
 
 
 def unit_forward(tokens_x, tokens_v, group):
@@ -101,7 +114,7 @@
 def cotangent_heads(out_cotangent, out_weight):
     summed = jnp.einsum(
         "tn,kn->tk",
-        lax.all_gather(out_cotangent, "head", axis=1, tiled=True),
+        gather_around(out_cotangent, "head", 1),
         out_weight,
         preferred_element_type=jnp.float32,
     )

time: 694 us -> 694 us (level)
  waiting for transfers between devices: 386 us -> 374 us
  local copies, waits for them, and re-layouts: 102 us -> 112 us
    all_gather x1 -> x0, waiting for transfers between devices: 50.2 us -> none  [cotangent_heads(): lax.all_gather(out_cotangent, 'head', axis=1, tiled=True)]
    ppermute x0 -> x3, waiting for transfers between devices: none -> 41.8 us  [the longest x2 41.7 us: gather_around(): earlier.append(lax.ppermute(earlier[-1], axis, up))]
    unnamed x13 -> x22, local copies, waits for them, and re-layouts: 2.59 us -> 9.78 us
  transfers between devices with their start and end apart: 8 -> 10, of which waited for: 6 -> 7; matrix products, arithmetic and copies ran while one was open for 33% -> 34% of each run, Pallas kernels for 0% -> 0%
where the time goes in v1:
time: 694 us; the launch traced here: 684 us
  waiting for transfers between devices  374 us (54%)
  local copies, waits for them, and re-layouts  112 us (16%)
  matrix products  109 us (16%)
  starting transfers between devices  50.2 us (7%)
  other arithmetic  23.5 us (3%)
  between operations  14.8 us (2%)
    all_to_all x1, waiting for transfers between devices, per_device(): lax.all_to_all(from_units(unit_gx, picking, seq_count), 'seq', split_axis...  88.9 us
    all_to_all x1, waiting for transfers between devices, per_device(): lax.all_to_all(send_x, 'seq', split_axis=0, concat_axis=0, tiled=True)  88.8 us
    all_to_all x1, waiting for transfers between devices, per_device(): lax.all_to_all(from_units(unit_gv, picking, seq_count), 'seq', split_axis...  78.5 us
    all_to_all x1, waiting for transfers between devices, per_device(): lax.all_to_all(to_slots(grad_attended, packing, seq_count), 'seq', split_...  54.1 us
    ppermute x2, waiting for transfers between devices, gather_around(): earlier.append(lax.ppermute(earlier[-1], axis, up))  41.7 us
    dynamic_slice x8, local copies, waits for them, and re-layouts, per_device(): lax.map(backward_unit, (unit_x, unit_v, unit_g, weights, unit_att))  40.2 us
    all_to_all x1, waiting for transfers between devices, per_device(): lax.all_to_all(send_v, 'seq', split_axis=0, concat_axis=0, tiled=True)  22 us
    mul x4, local copies, waits for them, and re-layouts, unit_backward(): grad_scores = weights * (grad_weights - row_delta)  21.5 us
  transfers between devices with their start and end apart: 10, of which 7 were waited for; matrix products, arithmetic and copies ran while one was open for 34% of the time, Pallas kernels for 0%

profile of v1, /device:TPU:16, one launch (start us, length us, event | category | flops | bytes accessed | tf_op | source)
XLA Modules:
  0.0 683.7 jit_solution(15613215929372805065)
XLA Ops:
  11.8 4.6 copy.60
  16.4 12.2 %all-to-all-start = ((bf16[64,256,128]{2,1,0:T(8,128)(2,1)}), bf16[64,256,128]{2,1,0:T(8,128)(2,1)}, u32[]{:S(2)}, u32[]{:S(2)}) async-start(bf16[64,256,128]{2,1,0:T(8,128)(2,1)} %bitcast.192), calls=%async_computation | async-start | bytes 8388608 | tf_op jit(solution)/shard_map/all_to_all | solution.py:160
  31.4 4.7 copy.64
  36.0 88.8 %all-to-all-done = bf16[64,256,128]{2,1,0:T(8,128)(2,1)} async-done(((bf16[64,256,128]{2,1,0:T(8,128)(2,1)}), bf16[64,256,128]{2,1,0:T(8,128)(2,1)}, u32[]{:S(2)}, u32[]{:S(2)}) %all-to-all-start) | async-done | bytes 4194336 | tf_op jit(solution)/shard_map/all_to_all | solution.py:160
  124.8 5.8 all-to-all-start.1
  130.7 1.5 collective-permute-start
  132.2 23.8 %collective-permute-done = bf16[1024,512]{1,0:T(8,128)(2,1)} collective-permute-done((bf16[1024,512]{1,0:T(8,128)(2,1)S(1)}, bf16[1024,512]{1,0:T(8,128)(2,1)}, u32[]{:S(2)}, u32[]{:S(2)}) %collective-permute-start) | collective-permute-done | bytes 1048608 | tf_op jit(solution)/shard_map/ppermute | solution.py:17
  162.3 18.0 %collective-permute-done.1 = bf16[1024,512]{1,0:T(8,128)(2,1)} collective-permute-done((bf16[1024,512]{1,0:T(8,128)(2,1)}, bf16[1024,512]{1,0:T(8,128)(2,1)}, u32[]{:S(2)}, u32[]{:S(2)}) %collective-permute-start.1) | collective-permute-done | bytes 1048608 | tf_op jit(solution)/shard_map/ppermute | solution.py:17
  189.0 3.3 fusion.90
  195.1 4.6 copy.73
  199.7 4.8 fusion.72
  204.9 22.0 %all-to-all-done.1 = bf16[64,256,128]{2,1,0:T(8,128)(2,1)} async-done(((bf16[64,256,128]{2,1,0:T(8,128)(2,1)}), bf16[64,256,128]{2,1,0:T(8,128)(2,1)}, u32[]{:S(2)}, u32[]{:S(2)}) %all-to-all-start.1) | async-done | bytes 4194336 | tf_op jit(solution)/shard_map/all_to_all | solution.py:161
  226.9 6.1 all-to-all-start.3
  233.0 4.8 fusion.75
  239.2 27.8 %while.24 = (s32[]{:T(128)}, f32[4,1024,1024]{1,2,0:T(8,128)}, f32[4,1024,128]{2,1,0:T(8,128)}, s32[4,8]{1,0:T(4,128)S(1)}, bf16[4,1024,128]{2,1,0:T(8,128)(2,1)S(1)}, /*index=5*/bf16[4,1024,128]{2,1,0:T(8,128)(2,1)}, s32[]{:T(128)}) while((s32[]{:T(128)}, f32[4,1024,1024]{1,2,0:T(8,128)}, f32[4,1024,128]{2,1,0:T(8,128)}, ...), condition=%wide.region_8.9_spmd, body=%wide.region_5.8_spmd.sunk | while | flops 550500352 | bytes 22062772 | solution.py:165
  241.0 2.5 bitcast_dynamic-update-slice_fusion.2
  243.5 2.6 fusion.165
  247.9 2.5 bitcast_dynamic-update-slice_fusion.2
  250.5 2.6 fusion.165
  254.9 2.5 bitcast_dynamic-update-slice_fusion.2
  257.4 2.6 fusion.165
  261.9 2.5 bitcast_dynamic-update-slice_fusion.2
  264.4 2.6 fusion.165
  266.9 2.1 convert_element_type.93
  270.4 4.7 copy.68
  275.1 54.1 %all-to-all-done.3 = bf16[64,256,128]{2,1,0:T(8,128)(2,1)} async-done(((bf16[64,256,128]{2,1,0:T(8,128)(2,1)}), bf16[64,256,128]{2,1,0:T(8,128)(2,1)}, u32[]{:S(2)}, u32[]{:S(2)}) %all-to-all-start.3) | async-done | bytes 4194336 | tf_op jit(solution)/shard_map/all_to_all | solution.py:176
  329.2 5.8 all-to-all-start.2
  335.0 4.8 fusion.78
  340.3 112.8 %while.25 = (s32[]{:T(128)}, bf16[4,1024,128]{2,1,0:T(8,128)(2,1)}, bf16[4,1024,128]{2,1,0:T(8,128)(2,1)}, f32[4,1024,1024]{1,2,0:T(8,128)}, bf16[4,1024,128]{2,...) while((s32[]{:T(128)}, bf16[4,1024,128]{2,1,0:T(8,128)(2,1)}, ...), condition=%wide.region_12.13_spmd, body=%wide.region_10.12_spmd.sunk | while | flops 811334656 | bytes 65285248 | solution.py:180
  341.5 4.7 constant_dynamic-slice_fusion.3
  346.3 5.3 copy.159
  351.6 4.9 bitcast_multiply_fusion.3
  356.5 5.4 copy.160
  361.9 5.1 fusion.173
  369.7 4.7 constant_dynamic-slice_fusion.3
  374.5 5.3 copy.159
  379.8 4.9 bitcast_multiply_fusion.3
  384.7 5.4 copy.160
  390.1 5.1 fusion.173
  397.9 4.7 constant_dynamic-slice_fusion.3
  402.7 5.3 copy.159
  408.0 4.9 bitcast_multiply_fusion.3
  412.9 5.4 copy.160
  418.3 5.1 fusion.173
  423.4 1.5 fusion.174
  426.1 4.7 constant_dynamic-slice_fusion.3
  430.9 5.3 copy.159
  436.2 4.9 bitcast_multiply_fusion.3
  441.1 5.4 copy.160
  446.5 5.1 fusion.173
  453.1 2.6 convolution_convert_fusion.2
  455.7 4.7 copy.78
  460.3 10.9 %all-to-all-start.4 = ((bf16[64,256,128]{2,1,0:T(8,128)(2,1)}), bf16[64,256,128]{2,1,0:T(8,128)(2,1)}, u32[]{:S(2)}, u32[]{:S(2)}) async-start(bf16[64,256,128]{2,1,0:T(8,128)(2,1)} %bitcast.191), calls=%async_computation.5 | async-start | bytes 8388608 | tf_op jit(solution)/shard_map/all_to_all | solution.py:182
  471.3 2.6 convolution_convert_fusion.1
  473.9 4.7 copy.82
  478.6 88.9 %all-to-all-done.4 = bf16[64,256,128]{2,1,0:T(8,128)(2,1)} async-done(((bf16[64,256,128]{2,1,0:T(8,128)(2,1)}), bf16[64,256,128]{2,1,0:T(8,128)(2,1)}, u32[]{:S(2)}, u32[]{:S(2)}) %all-to-all-start.4) | async-done | bytes 4194336 | tf_op jit(solution)/shard_map/all_to_all | solution.py:182
  567.5 5.8 all-to-all-start.5
  573.4 4.8 fusion.99
  578.2 2.0 copy.71
  580.2 5.6 convolution_convert_fusion
  585.8 4.8 fusion.96
  591.0 78.5 %all-to-all-done.5 = bf16[64,256,128]{2,1,0:T(8,128)(2,1)} async-done(((bf16[64,256,128]{2,1,0:T(8,128)(2,1)}), bf16[64,256,128]{2,1,0:T(8,128)(2,1)}, u32[]{:S(2)}, u32[]{:S(2)}) %all-to-all-start.5) | async-done | bytes 4194336 | tf_op jit(solution)/shard_map/all_to_all | solution.py:185
  669.5 4.8 fusion.93
  674.8 1.7 copy_bitcast_fusion
  (98 shorter events, 46.2 us)
Async XLA Ops:
  7.2 181.8 %copy-start = (bf16[512,2048]{1,0:T(8,128)(2,1)S(1)}, bf16[512,2048]{1,0:T(8,128)(2,1)}, u32[]{:S(2)}) copy-start(bf16[512,2048]{1,0:T(8,128)(2,1)} %param.11) | copy-start | bytes 6291460
  9.0 184.6 %copy-start.4 = (s32[8,4]{0,1:T(4,128)}, s32[8,4]{0,1:T(4,128)S(1)}, u32[]{:S(2)}) copy-start(s32[8,4]{0,1:T(4,128)S(1)} %copy.58) | copy-start | bytes 388
  16.4 108.4 %all-to-all-start = ((bf16[64,256,128]{2,1,0:T(8,128)(2,1)}), bf16[64,256,128]{2,1,0:T(8,128)(2,1)}, u32[]{:S(2)}, u32[]{:S(2)}) async-start(bf16[64,256,128]{2,1,0:T(8,128)(2,1)} %bitcast.192), calls=%async_computation | async-start | bytes 8388608 | tf_op jit(solution)/shard_map/all_to_all | solution.py:160
  124.8 5.8 copy-start.3
  124.8 37.2 %copy-start.6 = (s32[512,4]{0,1:T(4,128)S(1)}, s32[512,4]{0,1:T(4,128)}, u32[]{:S(2)}) copy-start(s32[512,4]{0,1:T(4,128)} %param.13) | copy-start | bytes 24580
  124.8 102.0 %all-to-all-start.1 = ((bf16[64,256,128]{2,1,0:T(8,128)(2,1)}), bf16[64,256,128]{2,1,0:T(8,128)(2,1)}, u32[]{:S(2)}, u32[]{:S(2)}) async-start(bf16[64,256,128]{2,1,0:T(8,128)(2,1)} %bitcast.187), calls=%async_computation.1 | async-start | bytes 8388608 | tf_op jit(solution)/shard_map/all_to_all | solution.py:161
  130.7 25.3 %collective-permute-start = (bf16[1024,512]{1,0:T(8,128)(2,1)S(1)}, bf16[1024,512]{1,0:T(8,128)(2,1)}, u32[]{:S(2)}, u32[]{:S(2)}) collective-permute-start(bf16[1024,512]{1,0:T(8,128)(2,1)S(1)} %copy-done.3), channel_id=1, source_target_pairs={{0,1},{1,2},{2,3},{3,0},{4,5},{5,6},{6,7},{7,4},{8,9},{9,10},{10,1... | collective-permute-start | bytes 3145736 | tf_op jit(solution)/shard_map/ppermute | solution.py:17
  155.9 24.4 %collective-permute-start.1 = (bf16[1024,512]{1,0:T(8,128)(2,1)}, bf16[1024,512]{1,0:T(8,128)(2,1)}, u32[]{:S(2)}, u32[]{:S(2)}) collective-permute-start(bf16[1024,512]{1,0:T(8,128)(2,1)} %collective-permute-done), channel_id=1, source_target_pairs={{0,1},{1,2},{2,3},{3,0},{4,5},{5,6},{6,7},{7,4},{8,9},{9,10},{10,1... | collective-permute-start | bytes 3145736 | tf_op jit(solution)/shard_map/ppermute | solution.py:17
  157.2 26.0 %collective-permute-start.2 = (bf16[1024,512]{1,0:T(8,128)(2,1)S(1)}, bf16[1024,512]{1,0:T(8,128)(2,1)}, u32[]{:S(2)}, u32[]{:S(2)}) collective-permute-start(bf16[1024,512]{1,0:T(8,128)(2,1)S(1)} %copy-done.3), channel_id=1, source_target_pairs={{0,3},{1,0},{2,1},{3,2},{4,7},{5,4},{6,5},{7,6},{8,11},{9,8},{10,9... | collective-permute-start | bytes 3145736 | tf_op jit(solution)/shard_map/ppermute | solution.py:19
  226.9 102.3 %all-to-all-start.3 = ((bf16[64,256,128]{2,1,0:T(8,128)(2,1)}), bf16[64,256,128]{2,1,0:T(8,128)(2,1)}, u32[]{:S(2)}, u32[]{:S(2)}) async-start(bf16[64,256,128]{2,1,0:T(8,128)(2,1)} %bitcast.188), calls=%async_computation.4 | async-start | bytes 8388608 | tf_op jit(solution)/shard_map/all_to_all | solution.py:176
  266.9 3.5 copy-start.2
  329.2 131.2 %all-to-all-start.2 = ((bf16[64,256,128]{2,1,0:T(8,128)(2,1)}), bf16[64,256,128]{2,1,0:T(8,128)(2,1)}, u32[]{:S(2)}, u32[]{:S(2)}) async-start(bf16[64,256,128]{2,1,0:T(8,128)(2,1)} %bitcast.189), calls=%async_computation.2 | async-start | bytes 8388608 | tf_op jit(solution)/shard_map/all_to_all | solution.py:166
  361.9 5.1 copy-start.1
  390.1 5.1 copy-start.1
  418.3 5.1 copy-start.1
  446.5 5.1 copy-start.1
  460.3 107.1 %all-to-all-start.4 = ((bf16[64,256,128]{2,1,0:T(8,128)(2,1)}), bf16[64,256,128]{2,1,0:T(8,128)(2,1)}, u32[]{:S(2)}, u32[]{:S(2)}) async-start(bf16[64,256,128]{2,1,0:T(8,128)(2,1)} %bitcast.191), calls=%async_computation.5 | async-start | bytes 8388608 | tf_op jit(solution)/shard_map/all_to_all | solution.py:182
  567.5 5.9 copy-start.5
  567.5 102.0 %all-to-all-start.5 = ((bf16[64,256,128]{2,1,0:T(8,128)(2,1)}), bf16[64,256,128]{2,1,0:T(8,128)(2,1)}, u32[]{:S(2)}, u32[]{:S(2)}) async-start(bf16[64,256,128]{2,1,0:T(8,128)(2,1)} %bitcast.190), calls=%async_computation.6 | async-start | bytes 8388608 | tf_op jit(solution)/shard_map/all_to_all | solution.py:185
  573.3 103.2 %reduce-scatter.2.cloned.1.call-start = ((), (), s32[]{:S(2)}) async-start(), calls=%async_computation.7 | async-start | bytes 5242880 | tf_op jit(solution)/shard_map/reduce_scatter | solution.py:109
Sparse Core Ops, SparseCore 0:
  585.9 48.8 reduce-scatter.1
